TPU v7x, 32 devices: a whole 2x2x4 slice. The times are simulated.
32 devices in a mesh: pipe: 4 (over z), seq: 2 (over core), tp: 4 (over y, x).
Axes of the slice: x: 2, y: 2, z: 4, core: 2. Of those that a mesh axis runs over, the one named last changes fastest.
Arguments:
- in_flight: bfloat16 [4, 128, 4096], P('pipe', 'tp', 'seq'), may hold values from -15 to 15
- arriving: bfloat16 [1, 128, 4096], P(None, 'tp', 'seq'), may hold values from -15 to 15
- norm_gain: bfloat16 [4, 4096], P('pipe', 'seq'), may hold values from 0.099609375 to 1.8984375
- gate_weight: bfloat16 [4, 4096, 5504], P('pipe', 'seq', 'tp'), may hold values from -0.09375 to 0.09375
- up_weight: bfloat16 [4, 4096, 5504], P('pipe', 'seq', 'tp'), may hold values from -0.09375 to 0.09375
- down_weight: bfloat16 [4, 5504, 4096], P('pipe', 'tp', 'seq'), may hold values from -0.078125 to 0.078125
Outputs:
- produced: bfloat16 [2, 4, 128, 4096], P(None, 'pipe', 'tp', 'seq')
All inputs are finite; a program needn't handle non-finite values.
Results may differ from a plain program's by a relative error of at most 0.015.
Values may be sent and summed in bfloat16 or wider, within the bound.
A program may use at most 64 MiB of HBM per device.

v0:
```python
import functools

import jax
import jax.numpy as jnp
from jax import lax
from jax.experimental import pallas as pl
from jax.experimental.pallas import tpu as pltpu
from jax.sharding import PartitionSpec as P

epsilon = 1e-05
MESH = pl.DeviceIdType.MESH
F32, BF16 = jnp.float32, jnp.bfloat16


def pieces(total, step):
    return [(at, min(step, total - at)) for at in range(0, total, step)]


def times(a, b):
    return lax.dot_general(a, b, (((1,), (1,)), ((), ())), preferred_element_type=F32)


def partner(me, k, n):
    if n & (n - 1):
        raise ValueError("axis size")
    result, bit = 0, 1
    while bit < n:
        digit = (me // bit) % 2
        if k & bit:
            digit = 1 - digit
        result = result + digit * bit
        bit *= 2
    return result


def body(cfg, *refs):
    T, R, DL, F, J, CW, NP, NS, NT, hidden_parts = cfg
    NF = len(hidden_parts)
    M = R * NT
    refs = list(refs)
    in_flight, arriving, gain, gate_w, up_w, down_w, out = refs[:7]
    (xin, xg, gate_v, up_v, down_v, acc_g, acc_u, acc_y, sq, sq_recv, rs_send, rs_recv, made) = refs[7:20]
    ex_send = refs[20:20 + NF]
    ex_recv = refs[20 + NF:20 + 2 * NF]
    (w_sem, d_sem, x_sem, z_sem, ag_s, ag_r, rs_s, rs_r, sq_s, sq_r, ex_s, ex_r) = refs[20 + 2 * NF:]

    pipe, seq, tp = lax.axis_index("pipe"), lax.axis_index("seq"), lax.axis_index("tp")
    width = DL * NS

    def remote(src, dst, send, recv, where):
        return pltpu.make_async_remote_copy(
            src_ref=src, dst_ref=dst, send_sem=send, recv_sem=recv, device_id=where, device_id_type=MESH
        )

    def await_local(ref, sem):
        pltpu.make_async_copy(ref, ref, sem).wait()

    for j in range(J):
        pltpu.make_async_copy(in_flight.at[0, :, pl.ds(j * CW, CW)], xin.at[0, j], x_sem.at[0, j]).start()

    @pl.when(pipe == 0)
    def _():
        for t in range(1, T):
            for j in range(J):
                pltpu.make_async_copy(
                    arriving.at[t - 1, :, pl.ds(j * CW, CW)], xin.at[t, j], x_sem.at[t, j]
                ).start()

    for j in range(J):
        for which, (src, dst) in enumerate(((gate_w, gate_v), (up_w, up_v))):
            pltpu.make_async_copy(src.at[0, :, pl.ds(j * CW, CW)], dst.at[j], w_sem.at[which, j]).start()
    for n, (at, size) in enumerate(hidden_parts):
        pltpu.make_async_copy(down_w.at[0, pl.ds(at, size), :], down_v.at[pl.ds(at, size), :], d_sem.at[n]).start()

    barrier = pltpu.get_barrier_semaphore()
    for k in range(1, NT):
        pl.semaphore_signal(barrier, inc=1, device_id={"tp": partner(tp, k, NT)}, device_id_type=MESH)
    for k in range(1, NS):
        pl.semaphore_signal(barrier, inc=1, device_id={"seq": partner(seq, k, NS)}, device_id_type=MESH)

    @pl.when(pipe > 0)
    def _():
        pl.semaphore_signal(barrier, inc=1, device_id={"pipe": pipe - 1}, device_id_type=MESH)

    peers = NT - 1 + NS - 1

    @pl.when(pipe < NP - 1)
    def _():
        pl.semaphore_wait(barrier, peers + 1)

    @pl.when(pipe == NP - 1)
    def _():
        pl.semaphore_wait(barrier, peers)

    def gather_copy(t, j, k):
        return remote(
            xin.at[t, j], xg.at[t, j, pl.ds(k * R, R), :], ag_s.at[t, j, k - 1], ag_r.at[t, j, k - 1],
            {"tp": partner(tp, k, NT)},
        )

    def spread(t, j):
        await_local(xin.at[t, j], x_sem.at[t, j])
        for k in reversed(range(1, NT)):
            gather_copy(t, j, k).start()
        xg[t, j, 0:R, :] = xin[t, j]

    def shift_copy(t, j):
        return remote(made.at[t, j], xin.at[t + 1, j], z_sem.at[t, j], x_sem.at[t + 1, j], {"pipe": pipe + 1})

    def scatter_copy(t, j, k):
        return remote(
            rs_send.at[t, j, pl.ds(k * R, R), :], rs_recv.at[t, j, k - 1], rs_s.at[t, j, k - 1],
            rs_r.at[t, j, k - 1], {"tp": partner(tp, k, NT)},
        )

    def squares_copy(t, k):
        return remote(sq.at[t], sq_recv.at[t, k - 1], sq_s.at[t, k - 1], sq_r.at[t, k - 1], {"seq": partner(seq, k, NS)})

    def exchange_copy(t, n, k):
        return remote(
            ex_send[n].at[t], ex_recv[n].at[t, k - 1], ex_s.at[t, n, k - 1], ex_r.at[t, n, k - 1],
            {"seq": partner(seq, k, NS)},
        )

    for j in range(J):
        spread(0, j)

    def tick(t, carry):
        acc_g[...] = jnp.zeros_like(acc_g)
        acc_u[...] = jnp.zeros_like(acc_u)
        sq[t] = jnp.zeros((M, 128), F32)

        def arrive(j):
            for k in range(1, NT):
                await_local(xg.at[t, j, pl.ds(k * R, R), :], ag_r.at[t, j, k - 1])

            @pl.when(t == 0)
            def _():
                await_local(gate_v.at[j], w_sem.at[0, j])
                await_local(up_v.at[j], w_sem.at[1, j])

            wide = xg[t, j].astype(F32)
            scaled = (wide * gain[:, pl.ds(pl.multiple_of(j * CW, CW), CW)].astype(F32)).astype(BF16)
            square = wide * wide
            total = sq[t]
            for at in range(0, CW, 128):
                total = total + square[:, at:at + 128]
            sq[t] = total
            return scaled

        def some(j, c):
            scaled = arrive(j)
            for at, size in pieces(F, 256):
                for weight, acc in ((gate_v, acc_g), (up_v, acc_u)):
                    acc[:, at:at + size] += times(scaled, weight[j, at:at + size, :])
            return c

        if J > 1:
            lax.fori_loop(0, J - 1, some, 0)
        scaled = arrive(J - 1)
        for k in range(1, NS):
            squares_copy(t, k).start()
        for n, (base, length) in enumerate(hidden_parts):
            for at, size in pieces(length, 256):
                for which, (weight, acc) in enumerate(((gate_v, acc_g), (up_v, acc_u))):
                    value = acc[:, base + at:base + at + size] + times(
                        scaled, weight[J - 1, base + at:base + at + size, :]
                    )
                    acc[:, base + at:base + at + size] = value
                    ex_send[n][t, which, :, at:at + size] = value.astype(BF16)
            for k in range(1, NS):
                exchange_copy(t, n, k).start()

        total = sq[t]
        for k in range(1, NS):
            await_local(sq_recv.at[t, k - 1], sq_r.at[t, k - 1])
            total = total + sq_recv[t, k - 1]
        inverse = lax.rsqrt(jnp.sum(total, axis=1, keepdims=True) / width + epsilon)

        for n, (base, length) in enumerate(hidden_parts):
            for k in range(1, NS):
                await_local(ex_recv[n].at[t, k - 1], ex_r.at[t, n, k - 1])

            @pl.when(t == 0)
            def _():
                await_local(down_v.at[pl.ds(base, length), :], d_sem.at[n])

            gate = acc_g[:, base:base + length]
            up = acc_u[:, base:base + length]
            for k in range(1, NS):
                gate = gate + ex_recv[n][t, k - 1, 0].astype(F32)
                up = up + ex_recv[n][t, k - 1, 1].astype(F32)
            hidden = (jax.nn.silu(gate * inverse) * (up * inverse)).astype(BF16)
            last = n == NF - 1
            for j in range(J):
                for at, size in pieces(CW, 256):
                    lo = j * CW + at
                    value = jnp.dot(hidden, down_v[base:base + length, lo:lo + size], preferred_element_type=F32)
                    if n > 0:
                        value = value + acc_y[:, lo:lo + size]
                    if last:
                        rs_send[t, j, :, at:at + size] = value.astype(BF16)
                    else:
                        acc_y[:, lo:lo + size] = value
                if last:
                    for k in reversed(range(1, NT)):
                        scatter_copy(t, j, k).start()

        def finish(j):
            branch = rs_send[t, j, 0:R, :].astype(F32)
            for k in range(1, NT):
                await_local(rs_recv.at[t, j, k - 1], rs_r.at[t, j, k - 1])
                branch = branch + rs_recv[t, j, k - 1].astype(F32)
            produced = (xin[t, j].astype(F32) + branch).astype(BF16)
            out[t, :, j * CW:(j + 1) * CW] = produced

            @pl.when((t < T - 1) & (pipe < NP - 1))
            def _():
                made[t, j] = produced
                shift_copy(t, j).start()

        for j in range(J):
            finish(j)
            if j > 0:
                @pl.when(t < T - 1)
                def _():
                    spread(t + 1, j - 1)

        @pl.when(t < T - 1)
        def _():
            spread(t + 1, J - 1)

        return carry

    lax.fori_loop(0, T, tick, 0)

    def sent(t, carry):
        for j in range(J):
            for k in range(1, NT):
                gather_copy(t, j, k).wait_send()
                scatter_copy(t, j, k).wait_send()

            @pl.when((t < T - 1) & (pipe < NP - 1))
            def _():
                shift_copy(t, j).wait_send()
        for k in range(1, NS):
            squares_copy(t, k).wait_send()
            for n in range(NF):
                exchange_copy(t, n, k).wait_send()
        return carry

    lax.fori_loop(0, T, sent, 0)


def solution(mesh):
    NP, NS, NT = mesh.shape["pipe"], mesh.shape["seq"], mesh.shape["tp"]

    def shards(in_flight, arriving, norm_gain, gate_weight, up_weight, down_weight):
        T = arriving.shape[0] + 1
        R, DL = in_flight.shape[1:]
        F = gate_weight.shape[2]
        CW = min(512, DL)
        J = DL // CW
        M = R * NT
        parts = pieces(F, 512)
        NF = len(parts)
        cfg = (T, R, DL, F, J, CW, NP, NS, NT, parts)
        hbm = pl.BlockSpec(memory_space=pltpu.HBM)
        vmem = pl.BlockSpec(memory_space=pltpu.VMEM)
        dma = pltpu.SemaphoreType.DMA
        ps = max(NS - 1, 1)
        scratch = [
            pltpu.VMEM((T, J, R, CW), BF16),
            pltpu.VMEM((T, J, M, CW), BF16),
            pltpu.VMEM((J, F, CW), BF16),
            pltpu.VMEM((J, F, CW), BF16),
            pltpu.VMEM((F, DL), BF16),
            pltpu.VMEM((M, F), F32),
            pltpu.VMEM((M, F), F32),
            pltpu.VMEM((M, DL), F32),
            pltpu.VMEM((T, M, 128), F32),
            pltpu.VMEM((T, ps, M, 128), F32),
            pltpu.VMEM((T, J, M, CW), BF16),
            pltpu.VMEM((T, J, NT - 1, R, CW), BF16),
            pltpu.VMEM((T, J, R, CW), BF16),
        ]
        scratch += [pltpu.VMEM((T, 2, M, size), BF16) for _, size in parts]
        scratch += [pltpu.VMEM((T, ps, 2, M, size), BF16) for _, size in parts]
        scratch += [
            dma((2, J)), dma((NF,)), dma((T, J)), dma((T, J)),
            dma((T, J, NT - 1)), dma((T, J, NT - 1)), dma((T, J, NT - 1)), dma((T, J, NT - 1)),
            dma((T, ps)), dma((T, ps)), dma((T, NF, ps)), dma((T, NF, ps)),
        ]
        flops = 2 * T * M * DL * F * 3
        made = pl.pallas_call(
            functools.partial(body, cfg),
            out_shape=jax.ShapeDtypeStruct((T, R, DL), BF16),
            in_specs=[hbm, hbm, vmem, hbm, hbm, hbm],
            out_specs=vmem,
            scratch_shapes=scratch,
            compiler_params=pltpu.CompilerParams(
                collective_id=0, has_side_effects=True, vmem_limit_bytes=56 * 1024 * 1024
            ),
            cost_estimate=pl.CostEstimate(flops=flops, bytes_accessed=6 * DL * F, transcendentals=T * M * F),
            name="relay",
        )(in_flight, arriving, norm_gain, jnp.swapaxes(gate_weight, 1, 2), jnp.swapaxes(up_weight, 1, 2), down_weight)
        return made[:, None]

    placed = (
        P("pipe", "tp", "seq"),
        P(None, "tp", "seq"),
        P("pipe", "seq"),
        P("pipe", "seq", "tp"),
        P("pipe", "seq", "tp"),
        P("pipe", "tp", "seq"),
    )
    return jax.shard_map(
        shards, mesh=mesh, in_specs=placed, out_specs=P(None, "pipe", "tp", "seq"), check_vma=False
    )
```

profile of v0, /device:TPU:0, one launch (start us, length us, event | category | flops | bytes accessed | tf_op | source)
XLA Modules:
  0.0 42.8 jit_solution(861109108846229887)
XLA Ops:
  0.0 41.2 %relay.1 = bf16[2,32,2048]{2,1,0:T(8,128)(2,1)} custom-call(bf16[1,32,2048]{2,1,0:T(8,128)(2,1)} %refs_0_.1, bf16[1,32,2048]{2,1,0:T(8,128)(2,1)} %refs_1_.1, bf16[1,2048]{1,0:T(2,128)(2,1)} %refs_2_.1, bf16[1,1376,2048]{2,1,0:T(8,128)(2,1)} %bitcast.5, bf16[1,1376,2048]{2,1,0:T(8,128)(2,1)} %bitcast.6, bf16[1,1376,2048]{2,1,0:T(8,128)(2,1)} %refs_5_.1), custom_call_target="tpu_custom_call" | custom-call | flops 4328521728 | bytes 16908288 | tf_op jit(solution)/shard_map/relay/pallas_call | solution.py:295
  41.2 1.7 %copy.9 = bf16[2,1,32,2048]{3,2,1,0:T(8,128)(2,1)} copy(bf16[2,1,32,2048]{3,2,1,0:T(8,128)(2,1)} %bitcast.7) | data formatting | bytes 524288
where the time goes:
time: 43.1 us; the launch traced here: 42.8 us
  Pallas kernels  41.2 us (96%)
  local copies, waits for them, and re-layouts  1.67 us (4%)
    pallas_call x1, Pallas kernels, shards(): pl.pallas_call(functools.partial(body, cfg), out_shape=jax.ShapeDtypeStru...  41.2 us
    unnamed x1, local copies, waits for them, and re-layouts  1.67 us

commit v1 on v0

--- a/solution.py
+++ b/solution.py
@@ -294,7 +294,7 @@
         flops = 2 * T * M * DL * F * 3
         made = pl.pallas_call(
             functools.partial(body, cfg),
-            out_shape=jax.ShapeDtypeStruct((T, R, DL), BF16),
+            out_shape=pltpu.VMEM((T, R, DL), BF16),
             in_specs=[hbm, hbm, vmem, hbm, hbm, hbm],
             out_specs=vmem,
             scratch_shapes=scratch,

time: 43.1 us -> 41.4 us (0.961)
  local copies, waits for them, and re-layouts: 1.67 us -> 0.71 us
  Pallas kernels: 41.2 us -> 40.5 us
    unnamed x1, local copies, waits for them, and re-layouts: 1.67 us -> 0.71 us
    pallas_call x1, Pallas kernels: 41.2 us -> 40.5 us  [shards(): pl.pallas_call(functools.partial(body, cfg), out_shape=pltpu.VMEM((T, R,...]
where the time goes in v1:
time: 41.4 us; the launch traced here: 41.2 us
  Pallas kernels  40.5 us (98%)
  local copies, waits for them, and re-layouts  0.71 us (2%)
    pallas_call x1, Pallas kernels, shards(): pl.pallas_call(functools.partial(body, cfg), out_shape=pltpu.VMEM((T, R,...  40.5 us

profile of v1, /device:TPU:0, one launch (start us, length us, event | category | flops | bytes accessed | tf_op | source)
XLA Modules:
  0.0 41.2 jit_solution(4284673429752216654)
XLA Ops:
  0.0 40.5 %relay.1 = bf16[2,32,2048]{2,1,0:T(8,128)(2,1)S(1)} custom-call(bf16[1,32,2048]{2,1,0:T(8,128)(2,1)} %refs_0_.1, bf16[1,32,2048]{2,1,0:T(8,128)(2,1)} %refs_1_.1, bf16[1,2048]{1,0:T(2,128)(2,1)} %refs_2_.1, bf16[1,1376,2048]{2,1,0:T(8,128)(2,1)} %bitcast.6, bf16[1,1376,2048]{2,1,0:T(8,128)(2,1)} %bitcast.7, bf16[1,1376,2048]{2,1,0:T(8,128)(2,1)} %refs_5_.1), custom_call_target="tpu_custom_call" | custom-call | flops 4328521728 | bytes 16908288 | tf_op jit(solution)/shard_map/relay/pallas_call | solution.py:295
  40.5 0.7 %copy.9 = bf16[2,1,32,2048]{3,2,1,0:T(8,128)(2,1)} copy(bf16[2,1,32,2048]{3,2,1,0:T(8,128)(2,1)S(1)} %bitcast.5) | data formatting | bytes 524288

commit v2 on v1

v2 whole, which is shorter than its diff:
```python
import functools

import jax
import jax.numpy as jnp
from jax import lax
from jax.experimental import pallas as pl
from jax.experimental.pallas import tpu as pltpu
from jax.sharding import PartitionSpec as P

epsilon = 1e-05
MESH = pl.DeviceIdType.MESH
F32, BF16 = jnp.float32, jnp.bfloat16
COLUMNS = 512
PART = 512
BEFORE = 1


def pieces(total, step):
    return [(at, min(step, total - at)) for at in range(0, total, step)]


def times(a, b):
    return lax.dot_general(a, b, (((1,), (1,)), ((), ())), preferred_element_type=F32)


def partner(me, k, n):
    if n & (n - 1):
        raise ValueError("axis size")
    result, bit = 0, 1
    while bit < n:
        digit = (me // bit) % 2
        if k & bit:
            digit = 1 - digit
        result = result + digit * bit
        bit *= 2
    return result


def body(cfg, *refs):
    T, R, DL, F, CW, H, NP, NS, NT, parts = cfg
    J, RH, NF = DL // CW, R // H, len(parts)
    M = RH * NT
    refs = list(refs)
    in_flight, arriving, gain_in, gate_w, up_w, down_w, out = refs[:7]
    (gain, xg, gate_v, up_v, gate_t, up_t, down_v, acc_g, acc_u, acc_y, sq, sq_recv, rs_send, rs_recv) = refs[7:21]
    ex_send = refs[21:21 + NF]
    ex_recv = refs[21 + NF:21 + 2 * NF]
    (g_sem, w_sem, d_sem, x_sem, z_sem, ag_s, ag_r, rs_s, rs_r, sq_s, sq_r, ex_s, ex_r) = refs[21 + 2 * NF:]

    pipe, seq, tp = lax.axis_index("pipe"), lax.axis_index("seq"), lax.axis_index("tp")
    width = DL * NS

    def remote(src, dst, send, recv, where):
        return pltpu.make_async_remote_copy(
            src_ref=src, dst_ref=dst, send_sem=send, recv_sem=recv, device_id=where, device_id_type=MESH
        )

    def await_bytes(ref, sem):
        pltpu.make_async_copy(ref, ref, sem).wait()

    def own(t, h, j):
        return xg.at[t, j, 0, h]

    def others(t, h, j):
        return xg.at[t, j, pl.ds(1, NT - 1), h]

    for j in range(J):
        for h in range(H):
            pltpu.make_async_copy(
                in_flight.at[0, pl.ds(h * RH, RH), pl.ds(j * CW, CW)], own(0, h, j), x_sem.at[0, h, j]
            ).start()
    pltpu.make_async_copy(gain_in, gain, g_sem).start()
    for j in range(J):
        for which, (src, dst) in enumerate(((gate_w, gate_v), (up_w, up_v))):
            pltpu.make_async_copy(src.at[0, :, pl.ds(j * CW, CW)], dst.at[j], w_sem.at[which, j]).start()
    for n, (at, size) in enumerate(parts):
        pltpu.make_async_copy(down_w.at[0, pl.ds(at, size), :], down_v.at[pl.ds(at, size), :], d_sem.at[n]).start()

    @pl.when(pipe == 0)
    def _():
        for t in range(1, T):
            for h in range(H):
                for j in range(J):
                    pltpu.make_async_copy(
                        arriving.at[t - 1, pl.ds(h * RH, RH), pl.ds(j * CW, CW)], own(t, h, j), x_sem.at[t, h, j]
                    ).start()

    barrier = pltpu.get_barrier_semaphore()
    for k in range(1, NT):
        pl.semaphore_signal(barrier, inc=1, device_id={"tp": partner(tp, k, NT)}, device_id_type=MESH)
    for k in range(1, NS):
        pl.semaphore_signal(barrier, inc=1, device_id={"seq": partner(seq, k, NS)}, device_id_type=MESH)

    @pl.when(pipe > 0)
    def _():
        pl.semaphore_signal(barrier, inc=1, device_id={"pipe": pipe - 1}, device_id_type=MESH)

    peers = NT - 1 + NS - 1

    @pl.when(pipe < NP - 1)
    def _():
        pl.semaphore_wait(barrier, peers + 1)

    @pl.when(pipe == NP - 1)
    def _():
        pl.semaphore_wait(barrier, peers)

    def spread(t, h, j):
        await_bytes(own(t, h, j), x_sem.at[t, h, j])
        for k in reversed(range(1, NT)):
            remote(
                own(t, h, j), xg.at[t, j, k, h], ag_s.at[t, h, j], ag_r.at[t, h, j], {"tp": partner(tp, k, NT)}
            ).start()

    def spread_all(t, j):
        for h in range(H):
            await_bytes(own(t, h, j), x_sem.at[t, h, j])
        for k in reversed(range(1, NT)):
            remote(
                xg.at[t, j, 0], xg.at[t, j, k], ag_s.at[t, 0, j], ag_r.at[t, 0, j], {"tp": partner(tp, k, NT)}
            ).start()

    def shift_copy(t, h, j):
        return remote(
            out.at[t, pl.ds(h * RH, RH), pl.ds(j * CW, CW)], own(t + 1, h, j), z_sem.at[t, h, j],
            x_sem.at[t + 1, h, j], {"pipe": pipe + 1},
        )

    def squares_copy(t, h, k):
        return remote(
            sq.at[t, h], sq_recv.at[t, h, k - 1], sq_s.at[t, h, k - 1], sq_r.at[t, h, k - 1],
            {"seq": partner(seq, k, NS)},
        )

    def exchange_copy(t, h, n, k):
        return remote(
            ex_send[n].at[t, h], ex_recv[n].at[t, h, k - 1], ex_s.at[t, h, n, k - 1], ex_r.at[t, h, n, k - 1],
            {"seq": partner(seq, k, NS)},
        )

    def scale(x, j):
        wide = x.astype(F32)
        scaled = (wide * gain[:, pl.ds(pl.multiple_of(j * CW, CW), CW)].astype(F32)).astype(BF16)
        square = wide * wide
        total = square[:, 0:128]
        for at in range(128, CW, 128):
            total = total + square[:, at:at + 128]
        return scaled, total

    def turn(j):
        for which, (raw, turned) in enumerate(((gate_v, gate_t), (up_v, up_t))):
            for at in range(0, CW, 256):
                turned[j, at:at + 256, :] = jnp.transpose(raw[j, :, at:at + 256])

    def arrive_all(t, j):
        await_bytes(xg.at[t, j, pl.ds(1, NT - 1)], ag_r.at[t, 0, j])
        scaled, total = scale(xg[t, j].reshape(H * M, CW), j)
        total = total.reshape(NT, H, RH, 128)
        for h in range(H):
            sq[t, h] += total[:, h].reshape(M, 128)
        return scaled

    def arrive(t, h, j):
        await_bytes(others(t, h, j), ag_r.at[t, h, j])
        scaled, total = scale(xg[t, j, :, h].reshape(M, CW), j)
        sq[t, h] += total
        return scaled

    kinds = ((gate_t, acc_g), (up_t, acc_u))
    raws = ((gate_v, acc_g), (up_v, acc_u))

    def loaded(j):
        await_bytes(gate_v.at[j], w_sem.at[0, j])
        await_bytes(up_v.at[j], w_sem.at[1, j])

    def clear(t):
        acc_g[...] = jnp.zeros_like(acc_g)
        acc_u[...] = jnp.zeros_like(acc_u)
        for h in range(H):
            sq[t, h] = jnp.zeros((M, 128), F32)

    def project_all(t, j):
        scaled = arrive_all(t, j)
        for at, size in pieces(F, 256):
            for weight, acc in raws:
                acc[:, :, :, at:at + size] += times(scaled, weight[j, at:at + size, :]).reshape(NT, H, RH, size)

    def project(t, h, j):
        scaled = arrive(t, h, j)
        for at, size in pieces(F, 256):
            for weight, acc in kinds:
                acc[:, h, :, at:at + size] += jnp.dot(
                    scaled, weight[j, :, at:at + size], preferred_element_type=F32
                ).reshape(NT, RH, size)

    def last_all(t):
        scaled = arrive_all(t, J - 1)
        for h in range(H):
            for k in range(1, NS):
                squares_copy(t, h, k).start()
        for n, (base, length) in enumerate(parts):
            for at, size in pieces(length, 256):
                lo, hi = base + at, base + at + size
                for which, (weight, acc) in enumerate(raws):
                    value = acc[:, :, :, lo:hi] + times(scaled, weight[J - 1, lo:hi, :]).reshape(NT, H, RH, size)
                    acc[:, :, :, lo:hi] = value
                    rounded = value.astype(BF16)
                    for h in range(H):
                        ex_send[n][t, h, which, :, at:at + size] = rounded[:, h].reshape(M, size)
            for h in range(H):
                for k in range(1, NS):
                    exchange_copy(t, h, n, k).start()

    def project_last(t, h):
        scaled = arrive(t, h, J - 1)
        for k in range(1, NS):
            squares_copy(t, h, k).start()
        for n, (base, length) in enumerate(parts):
            for at, size in pieces(length, 256):
                lo, hi = base + at, base + at + size
                for which, (weight, acc) in enumerate(kinds):
                    value = acc[:, h, :, lo:hi].reshape(M, size) + jnp.dot(
                        scaled, weight[J - 1, :, lo:hi], preferred_element_type=F32
                    )
                    acc[:, h, :, lo:hi] = value.reshape(NT, RH, size)
                    ex_send[n][t, h, which, :, at:at + size] = value.astype(BF16)
            for k in range(1, NS):
                exchange_copy(t, h, n, k).start()

    def contract(t, h):
        total = sq[t, h]
        for k in range(1, NS):
            await_bytes(sq_recv.at[t, h, k - 1], sq_r.at[t, h, k - 1])
            total = total + sq_recv[t, h, k - 1]
        inverse = lax.rsqrt(jnp.sum(total, axis=1, keepdims=True) / width + epsilon)
        for n, (base, length) in enumerate(parts):
            for k in range(1, NS):
                await_bytes(ex_recv[n].at[t, h, k - 1], ex_r.at[t, h, n, k - 1])
            if h == 0 and isinstance(t, int):
                await_bytes(down_v.at[pl.ds(base, length), :], d_sem.at[n])
            gate = acc_g[:, h, :, base:base + length].reshape(M, length)
            up = acc_u[:, h, :, base:base + length].reshape(M, length)
            for k in range(1, NS):
                gate = gate + ex_recv[n][t, h, k - 1, 0].astype(F32)
                up = up + ex_recv[n][t, h, k - 1, 1].astype(F32)
            hidden = (jax.nn.silu(gate * inverse) * (up * inverse)).astype(BF16)
            last = n == NF - 1
            for j in range(J):
                for at, size in pieces(CW, 256):
                    lo = j * CW + at
                    value = jnp.dot(hidden, down_v[base:base + length, lo:lo + size], preferred_element_type=F32)
                    if n > 0:
                        value = value + acc_y[:, lo:lo + size]
                    if last:
                        rs_send[t, h, j, :, at:at + size] = value.astype(BF16)
                    else:
                        acc_y[:, lo:lo + size] = value
                if last:
                    for k in reversed(range(1, NT)):
                        remote(
                            rs_send.at[t, h, j, pl.ds(k * RH, RH), :], rs_recv.at[t, h, j, pl.ds((k - 1) * RH, RH), :],
                            rs_s.at[t, h, j], rs_r.at[t, h, j], {"tp": partner(tp, k, NT)},
                        ).start()

    def finish(t, h, j):
        await_bytes(rs_recv.at[t, h, j], rs_r.at[t, h, j])
        branch = rs_send[t, h, j, 0:RH, :].astype(F32)
        for k in range(1, NT):
            branch = branch + rs_recv[t, h, j, (k - 1) * RH:k * RH, :].astype(F32)
        produced = (xg[t, j, 0, h].astype(F32) + branch).astype(BF16)
        out[t, h * RH:(h + 1) * RH, j * CW:(j + 1) * CW] = produced

        @pl.when((t < T - 1) & (pipe < NP - 1))
        def _():
            shift_copy(t, h, j).start()

    for j in range(J):
        spread_all(0, j)
    await_bytes(gain, g_sem)
    clear(0)

    def opening(j, c):
        loaded(j)
        project_all(0, j)
        return c

    lax.fori_loop(0, J - 1, opening, 0)
    loaded(J - 1)
    last_all(0)

    def close(t, more):
        for h in range(H - 1):
            for j in range(J):
                finish(t, h, j)
        for j in range(J):
            finish(t, H - 1, j)
            if H > 1:
                @pl.when(more)
                def _():
                    spread(t + 1, 0, j)
        if H == 1:
            @pl.when(more)
            def _():
                for j in range(J):
                    spread(t + 1, 0, j)

    for h in range(H):
        contract(0, h)
    for j in range(J):
        turn(j)
    close(0, T > 1)

    def tick(t, carry):
        clear(t)

        def first(j, c):
            if H > 1:
                spread(t, 1, j)
            project(t, 0, j)
            return c

        lax.fori_loop(0, J - 1, first, 0)
        if H > 1:
            spread(t, 1, J - 1)
        project_last(t, 0)
        if H > 1:
            def second(j, c):
                project(t, 1, j)
                return c

            lax.fori_loop(0, BEFORE, second, 0)
            contract(t, 0)
            lax.fori_loop(BEFORE, J - 1, second, 0)
            project_last(t, 1)
        contract(t, H - 1)
        close(t, t < T - 1)
        return carry

    lax.fori_loop(1, T, tick, 0)

    for j in range(J):
        await_bytes(xg.at[0, j, pl.ds(1, NT - 1)], ag_s.at[0, 0, j])

    def sent(t, carry):
        for h in range(H):
            for j in range(J):
                @pl.when(t > 0)
                def _():
                    await_bytes(others(t, h, j), ag_s.at[t, h, j])

                await_bytes(rs_recv.at[t, h, j], rs_s.at[t, h, j])

                @pl.when((t < T - 1) & (pipe < NP - 1))
                def _():
                    shift_copy(t, h, j).wait_send()
            for k in range(1, NS):
                squares_copy(t, h, k).wait_send()
                for n in range(NF):
                    exchange_copy(t, h, n, k).wait_send()
        return carry

    lax.fori_loop(0, T, sent, 0)


def solution(mesh):
    NP, NS, NT = mesh.shape["pipe"], mesh.shape["seq"], mesh.shape["tp"]

    def shards(in_flight, arriving, norm_gain, gate_weight, up_weight, down_weight):
        T = arriving.shape[0] + 1
        R, DL = in_flight.shape[1:]
        F = gate_weight.shape[2]
        CW = min(COLUMNS, DL)
        J = DL // CW
        H = 2 if R % 32 == 0 else 1
        RH = R // H
        M = RH * NT
        parts = pieces(F, PART)
        NF = len(parts)
        cfg = (T, R, DL, F, CW, H, NP, NS, NT, parts)
        hbm = pl.BlockSpec(memory_space=pltpu.HBM)
        vmem = pl.BlockSpec(memory_space=pltpu.VMEM)
        dma = pltpu.SemaphoreType.DMA
        ps = max(NS - 1, 1)
        scratch = [
            pltpu.VMEM((1, DL), BF16),
            pltpu.VMEM((T, J, NT, H, RH, CW), BF16),
            pltpu.VMEM((J, F, CW), BF16),
            pltpu.VMEM((J, F, CW), BF16),
            pltpu.VMEM((J, CW, F), BF16),
            pltpu.VMEM((J, CW, F), BF16),
            pltpu.VMEM((F, DL), BF16),
            pltpu.VMEM((NT, H, RH, F), F32),
            pltpu.VMEM((NT, H, RH, F), F32),
            pltpu.VMEM((M, DL), F32),
            pltpu.VMEM((T, H, M, 128), F32),
            pltpu.VMEM((T, H, ps, M, 128), F32),
            pltpu.VMEM((T, H, J, M, CW), BF16),
            pltpu.VMEM((T, H, J, M - RH, CW), BF16),
        ]
        scratch += [pltpu.VMEM((T, H, 2, M, size), BF16) for _, size in parts]
        scratch += [pltpu.VMEM((T, H, ps, 2, M, size), BF16) for _, size in parts]
        scratch += [
            dma, dma((2, J)), dma((NF,)), dma((T, H, J)), dma((T, H, J)),
            dma((T, H, J)), dma((T, H, J)), dma((T, H, J)), dma((T, H, J)),
            dma((T, H, ps)), dma((T, H, ps)), dma((T, H, NF, ps)), dma((T, H, NF, ps)),
        ]
        flops = 2 * T * H * M * DL * F * 3
        made = pl.pallas_call(
            functools.partial(body, cfg),
            out_shape=pltpu.VMEM((T, R, DL), BF16),
            in_specs=[hbm, hbm, hbm, hbm, hbm, hbm],
            out_specs=vmem,
            scratch_shapes=scratch,
            compiler_params=pltpu.CompilerParams(
                collective_id=0, has_side_effects=True, vmem_limit_bytes=56 * 1024 * 1024
            ),
            cost_estimate=pl.CostEstimate(flops=flops, bytes_accessed=6 * DL * F, transcendentals=T * H * M * F),
            name="relay",
        )(in_flight, arriving, norm_gain, jnp.swapaxes(gate_weight, 1, 2), jnp.swapaxes(up_weight, 1, 2), down_weight)
        return made[:, None]

    placed = (
        P("pipe", "tp", "seq"),
        P(None, "tp", "seq"),
        P("pipe", "seq"),
        P("pipe", "seq", "tp"),
        P("pipe", "seq", "tp"),
        P("pipe", "tp", "seq"),
    )
    return jax.shard_map(
        shards, mesh=mesh, in_specs=placed, out_specs=P(None, "pipe", "tp", "seq"), check_vma=False
    )
```

time: 41.4 us -> 40.2 us (0.971)
  Pallas kernels: 40.5 us -> 39.3 us
    pallas_call x1, Pallas kernels: 40.5 us -> 39.3 us  [shards(): pl.pallas_call(functools.partial(body, cfg), out_shape=pltpu.VMEM((T, R,...]
where the time goes in v2:
time: 40.2 us; the launch traced here: 40 us
  Pallas kernels  39.3 us (98%)
  local copies, waits for them, and re-layouts  0.71 us (2%)
    pallas_call x1, Pallas kernels, shards(): pl.pallas_call(functools.partial(body, cfg), out_shape=pltpu.VMEM((T, R,...  39.3 us

profile of v2, /device:TPU:0, one launch (start us, length us, event | category | flops | bytes accessed | tf_op | source)
XLA Modules:
  0.0 40.0 jit_solution(16277486197486593188)
XLA Ops:
  0.0 39.3 %relay.1 = bf16[2,32,2048]{2,1,0:T(8,128)(2,1)S(1)} custom-call(bf16[1,32,2048]{2,1,0:T(8,128)(2,1)} %refs_0_.1, bf16[1,32,2048]{2,1,0:T(8,128)(2,1)} %refs_1_.1, bf16[1,2048]{1,0:T(2,128)(2,1)} %refs_2_.1, bf16[1,1376,2048]{2,1,0:T(8,128)(2,1)} %bitcast.6, bf16[1,1376,2048]{2,1,0:T(8,128)(2,1)} %bitcast.7, bf16[1,1376,2048]{2,1,0:T(8,128)(2,1)} %refs_5_.1), custom_call_target="tpu_custom_call" | custom-call | flops 4328521728 | bytes 16908288 | tf_op jit(solution)/shard_map/relay/pallas_call | solution.py:408
  39.3 0.7 %copy.9 = bf16[2,1,32,2048]{3,2,1,0:T(8,128)(2,1)} copy(bf16[2,1,32,2048]{3,2,1,0:T(8,128)(2,1)S(1)} %bitcast.5) | data formatting | bytes 524288

commit v3 on v2

--- a/solution.py
+++ b/solution.py
@@ -11,7 +11,7 @@
 MESH = pl.DeviceIdType.MESH
 F32, BF16 = jnp.float32, jnp.bfloat16
 COLUMNS = 512
-PART = 512
+PART = 1408
 BEFORE = 1
 
 
@@ -304,9 +304,11 @@
                 for j in range(J):
                     spread(t + 1, 0, j)
 
+    for j in range(J // 4):
+        turn(j)
     for h in range(H):
         contract(0, h)
-    for j in range(J):
+    for j in range(J // 4, J):
         turn(j)
     close(0, T > 1)
 
@@ -314,24 +316,23 @@
         clear(t)
 
         def first(j, c):
-            if H > 1:
-                spread(t, 1, j)
             project(t, 0, j)
             return c
 
-        lax.fori_loop(0, J - 1, first, 0)
         if H > 1:
-            spread(t, 1, J - 1)
+            for j in range(J):
+                spread(t, 1, j)
+        for j in range(J - 1):
+            first(j, 0)
         project_last(t, 0)
         if H > 1:
             def second(j, c):
                 project(t, 1, j)
                 return c
 
-            lax.fori_loop(0, BEFORE, second, 0)
+            [second(j, 0) for j in range(J - 1)]
+            project_last(t, 1)
             contract(t, 0)
-            lax.fori_loop(BEFORE, J - 1, second, 0)
-            project_last(t, 1)
         contract(t, H - 1)
         close(t, t < T - 1)
         return carry

time: 40.2 us -> 38.8 us (0.965)
  Pallas kernels: 39.3 us -> 38 us
    pallas_call x1, Pallas kernels: 39.3 us -> 38 us  [shards(): pl.pallas_call(functools.partial(body, cfg), out_shape=pltpu.VMEM((T, R,...]
where the time goes in v3:
time: 38.8 us; the launch traced here: 38.7 us
  Pallas kernels  38 us (98%)
  local copies, waits for them, and re-layouts  0.71 us (2%)
    pallas_call x1, Pallas kernels, shards(): pl.pallas_call(functools.partial(body, cfg), out_shape=pltpu.VMEM((T, R,...  38 us

profile of v3, /device:TPU:0, one launch (start us, length us, event | category | flops | bytes accessed | tf_op | source)
XLA Modules:
  0.0 38.7 jit_solution(5262571792462981797)
XLA Ops:
  0.0 38.0 %relay.1 = bf16[2,32,2048]{2,1,0:T(8,128)(2,1)S(1)} custom-call(bf16[1,32,2048]{2,1,0:T(8,128)(2,1)} %refs_0_.1, bf16[1,32,2048]{2,1,0:T(8,128)(2,1)} %refs_1_.1, bf16[1,2048]{1,0:T(2,128)(2,1)} %refs_2_.1, bf16[1,1376,2048]{2,1,0:T(8,128)(2,1)} %bitcast.6, bf16[1,1376,2048]{2,1,0:T(8,128)(2,1)} %bitcast.7, bf16[1,1376,2048]{2,1,0:T(8,128)(2,1)} %refs_5_.1), custom_call_target="tpu_custom_call" | custom-call | flops 4328521728 | bytes 16908288 | tf_op jit(solution)/shard_map/relay/pallas_call | solution.py:409
  38.0 0.7 %copy.9 = bf16[2,1,32,2048]{3,2,1,0:T(8,128)(2,1)} copy(bf16[2,1,32,2048]{3,2,1,0:T(8,128)(2,1)S(1)} %bitcast.5) | data formatting | bytes 524288

commit v4 on v3

--- a/solution.py
+++ b/solution.py
@@ -246,7 +246,7 @@
             hidden = (jax.nn.silu(gate * inverse) * (up * inverse)).astype(BF16)
             last = n == NF - 1
             for j in range(J):
-                for at, size in pieces(CW, 256):
+                for at, size in pieces(CW, 512):
                     lo = j * CW + at
                     value = jnp.dot(hidden, down_v[base:base + length, lo:lo + size], preferred_element_type=F32)
                     if n > 0:
@@ -306,9 +306,12 @@
 
     for j in range(J // 4):
         turn(j)
-    for h in range(H):
+    contract(0, 0)
+    for j in range(J // 4, J // 2):
+        turn(j)
+    for h in range(1, H):
         contract(0, h)
-    for j in range(J // 4, J):
+    for j in range(J // 2, J):
         turn(j)
     close(0, T > 1)
 

time: 38.8 us -> 38.8 us (level)
  no operation moved by 1% of the time
where the time goes in v4:
time: 38.8 us; the launch traced here: 38.7 us
  Pallas kernels  38 us (98%)
  local copies, waits for them, and re-layouts  0.71 us (2%)
    pallas_call x1, Pallas kernels, shards(): pl.pallas_call(functools.partial(body, cfg), out_shape=pltpu.VMEM((T, R,...  38 us

profile of v4, /device:TPU:0, one launch (start us, length us, event | category | flops | bytes accessed | tf_op | source)
XLA Modules:
  0.0 38.7 jit_solution(14742705024795513113)
XLA Ops:
  0.0 38.0 %relay.1 = bf16[2,32,2048]{2,1,0:T(8,128)(2,1)S(1)} custom-call(bf16[1,32,2048]{2,1,0:T(8,128)(2,1)} %refs_0_.1, bf16[1,32,2048]{2,1,0:T(8,128)(2,1)} %refs_1_.1, bf16[1,2048]{1,0:T(2,128)(2,1)} %refs_2_.1, bf16[1,1376,2048]{2,1,0:T(8,128)(2,1)} %bitcast.6, bf16[1,1376,2048]{2,1,0:T(8,128)(2,1)} %bitcast.7, bf16[1,1376,2048]{2,1,0:T(8,128)(2,1)} %refs_5_.1), custom_call_target="tpu_custom_call" | custom-call | flops 4328521728 | bytes 16908288 | tf_op jit(solution)/shard_map/relay/pallas_call | solution.py:412
  38.0 0.7 %copy.9 = bf16[2,1,32,2048]{3,2,1,0:T(8,128)(2,1)} copy(bf16[2,1,32,2048]{3,2,1,0:T(8,128)(2,1)S(1)} %bitcast.5) | data formatting | bytes 524288
